TPU v7x, 512 devices: a whole 4x8x8 slice. The times are simulated.
512 devices in a mesh: prow: 16 (over z_lo, x, core), pcol: 32 (over y, z_hi).
Axes of the slice: x: 4, y: 8, z: 8 (z_hi: 4, z_lo: 2; z = z_hi * 2 + z_lo), core: 2. Of those that a mesh axis runs over, the one named last changes fastest.
Arguments:
- matrix: float32 [6, 16, 128, 3, 32, 128], P(None, 'prow', None, None, 'pcol'), may hold values from -1 to 40, as said below
- row_codes: int32 [6, 16, 128], P(None, 'prow'), may hold values from 1 to 8
- col_codes: int32 [3, 32, 128], P(None, 'pcol'), may hold values from 1 to 8
- fault_tiles: int32 [96, 2], replicated, may hold values from 0 to 95, as said below
- fault_cells: int32 [96, 2], replicated, may hold values from 0 to 127
- fault_bits: int32 [96], replicated, may hold values from 1 to 2
Outputs:
- factored: float32 [6, 16, 128, 3, 32, 128], P(None, 'prow', None, None, 'pcol')
- col_check: float32 [3, 32, 128], P(None, 'pcol')
- row_check: float32 [6, 16, 128], P(None, 'prow')
- col_flags: float32 [3, 32], P(None, 'pcol')
- row_flags: float32 [6, 16], P(None, 'prow')
Inputs may be any that keep to these rules, and one draw needn't show every extreme that they name: `matrix`: symmetric positive definite. `fault_tiles`: each tile row index appears in exactly one fault, and so does each tile column index.
All inputs are finite; a program needn't handle non-finite values.
Results may differ from a plain program's by a relative error of at most 0.0003.
Values sent between devices are 32-bit elements; how exact they have to be, the bound alone decides.
No kernel may reach another device: no remote copies, remote signals or barrier semaphores. Data moves between devices by JAX's collectives and lax.ppermute only.
A program may use at most 64 MiB of HBM per device.

v0:
```python
import jax
import jax.numpy as jnp
from jax import lax
from jax.sharding import PartitionSpec as P

STEPS = 2
precise = lax.Precision.HIGHEST


def broadcast(block, axis, holder):
    block = jnp.where(lax.axis_index(axis) == holder, block, jnp.zeros_like(block))
    return lax.psum(block, axis)


def factor_diagonal(diagonal):
    factor = jnp.linalg.cholesky(diagonal)
    identity = jnp.eye(diagonal.shape[0], dtype=jnp.float32)
    inverse = jax.scipy.linalg.solve_triangular(factor, identity, lower=True)
    return (factor, inverse)


def form_panel(col_blocks, tile_ids, factor, inverse, step_index):
    product = jnp.einsum("iab,cb->iac", col_blocks, inverse, precision=precise)
    chosen = jnp.where((tile_ids == step_index)[:, None, None], factor[None], 0.0)
    return jnp.where((tile_ids > step_index)[:, None, None], product, chosen)


def update_range(blocks, trailing_rows, trailing_cols):
    update = jnp.einsum("iab,jcb->iajc", trailing_rows, trailing_cols, precision=precise)
    return blocks - update


def local(matrix, row_codes, col_codes, fault_tiles, fault_cells, fault_bits):
    grid_rows = lax.axis_size("prow")
    grid_cols = lax.axis_size("pcol")
    grid_row = lax.axis_index("prow")
    grid_col = lax.axis_index("pcol")
    tile_rows, _, tile_size, tile_cols, _, _ = matrix.shape
    blocks = matrix.reshape(tile_rows, tile_size, tile_cols, tile_size)
    row_weights = row_codes.reshape(tile_rows, tile_size).astype(jnp.float32) * 0.25
    col_weights = col_codes.reshape(tile_cols, tile_size).astype(jnp.float32) * 0.25
    tile_row = jnp.arange(tile_rows, dtype=jnp.int32) * grid_rows + grid_row
    tile_col = jnp.arange(tile_cols, dtype=jnp.int32) * grid_cols + grid_col
    col_check = lax.psum(jnp.einsum("ia,iajc->jc", row_weights, blocks, precision=precise), "prow")
    row_check = lax.psum(jnp.einsum("iajc,jc->ia", blocks, col_weights, precision=precise), "pcol")
    magnitude = jnp.exp2(fault_bits.astype(jnp.float32) - 1.0)
    fault_rows = fault_tiles[:, 0] * tile_size + fault_cells[:, 0]
    fault_cols = fault_tiles[:, 1] * tile_size + fault_cells[:, 1]
    offsets = jnp.arange(tile_size, dtype=jnp.int32)
    local_rows = (tile_row[:, None] * tile_size + offsets[None, :]).reshape(-1)
    local_cols = (tile_col[:, None] * tile_size + offsets[None, :]).reshape(-1)
    hit_rows = (fault_rows[:, None] == local_rows[None, :]).astype(jnp.float32) * magnitude[:, None]
    hit_cols = (fault_cols[:, None] == local_cols[None, :]).astype(jnp.float32)
    faults_added = jnp.dot(hit_rows.T, hit_cols, precision=precise)
    blocks = blocks + faults_added.reshape(tile_rows, tile_size, tile_cols, tile_size)
    picked = (
        jnp.arange(tile_cols, dtype=jnp.int32) * (grid_cols // grid_rows) + grid_col // grid_rows
    )
    owner_row = grid_col % grid_rows

    def factor_panel(blocks, row_check, col_check, step_index):
        root_row = step_index % grid_rows
        root_col = step_index % grid_cols
        local_row = step_index // grid_rows
        local_col = step_index // grid_cols
        diagonal = broadcast(blocks[local_row, :, local_col, :], "prow", root_row)
        factor, inverse = factor_diagonal(diagonal)
        own_rows = form_panel(blocks[:, :, local_col, :], tile_row, factor, inverse, step_index)
        own_check = jnp.dot(inverse, col_check[local_col], precision=precise)
        panel_rows, new_check = (
            broadcast(own_rows, "pcol", root_col),
            broadcast(own_check, "pcol", root_col),
        )
        across = broadcast(jnp.take(panel_rows, picked, axis=0), "prow", owner_row)
        owner_col = grid_col == root_col
        shift_term = jnp.einsum("jab,ja->b", across, col_weights, precision=precise)
        shift_term = shift_term - jnp.where(owner_col, col_weights[local_col], 0.0)
        shift_vector = lax.psum(shift_term, "pcol")
        row_check = row_check - jnp.einsum("iab,b->ia", panel_rows, shift_vector, precision=precise)
        col_update = jnp.einsum("jab,b->ja", across, new_check, precision=precise)
        col_check = col_check - jnp.where((tile_col > step_index)[:, None], col_update, 0.0)
        col_check = col_check.at[local_col].set(
            jnp.where(owner_col, new_check, col_check[local_col])
        )
        trailing_rows = jnp.where((tile_row > step_index)[:, None, None], panel_rows, 0.0)
        trailing_cols = jnp.where((tile_col > step_index)[:, None, None], across, 0.0)
        return (panel_rows, trailing_rows, trailing_cols, row_check, col_check)

    current = factor_panel(blocks, row_check, col_check, 0)
    for step_index in range(STEPS):
        panel_rows, trailing_rows, trailing_cols, row_check, col_check = current
        blocks = update_range(blocks, trailing_rows, trailing_cols)
        if step_index + 1 < STEPS:
            current = factor_panel(blocks, row_check, col_check, step_index + 1)
        settle_blocks = blocks
        settle_local_col = step_index // grid_cols
        previous = settle_blocks[:, :, settle_local_col, :]
        settle_blocks = settle_blocks.at[:, :, settle_local_col, :].set(
            jnp.where(grid_col == step_index % grid_cols, panel_rows, previous)
        )
        cleared = (tile_row == step_index)[:, None, None, None] & (tile_col > step_index)[
            None, None, :, None
        ]
        blocks = jnp.where(cleared, 0.0, settle_blocks)
    col_found = lax.psum(jnp.einsum("ia,iajc->jc", row_weights, blocks, precision=precise), "prow")
    row_found = lax.psum(jnp.einsum("iajc,jc->ia", blocks, col_weights, precision=precise), "pcol")
    col_flags = jnp.max(jnp.abs(col_check - col_found), axis=1)
    row_flags = jnp.max(jnp.abs(row_check - row_found), axis=1)
    return (
        blocks.reshape(matrix.shape),
        col_check.reshape(tile_cols, 1, tile_size),
        row_check.reshape(tile_rows, 1, tile_size),
        col_flags.reshape(tile_cols, 1),
        row_flags.reshape(tile_rows, 1),
    )


def solution(mesh):
    return jax.shard_map(
        local,
        mesh=mesh,
        in_specs=(
            P(None, "prow", None, None, "pcol", None),
            P(None, "prow", None),
            P(None, "pcol", None),
            P(),
            P(),
            P(),
        ),
        out_specs=(
            P(None, "prow", None, None, "pcol", None),
            P(None, "pcol", None),
            P(None, "prow", None),
            P(None, "pcol"),
            P(None, "prow"),
        ),
        check_vma=False,
    )
```

profile of v0, /device:TPU:64, one launch (start us, length us, event | category | flops | bytes accessed | tf_op | source)
XLA Modules:
  0.0 1383.4 jit_solution(15013393687045354452)
XLA Ops:
  7.2 0.7 multiply_exponential_fusion
  8.1 0.8 add_bitcast_fusion.2
  8.8 0.7 fusion.15
  9.6 1.3 reshape.353
  10.9 0.3 copy-done.7
  11.2 0.9 copy.30
  12.1 1.7 bitcast_add_fusion
  13.8 0.6 fusion.42
  14.6 0.6 broadcast_compare_fusion.4
  15.2 0.6 broadcast_and_fusion
  15.9 118.3 %all-reduce.9.cloned.1.call-done = f32[128,128]{0,1:T(8,128)} async-done(((f32[128,128]{0,1:T(8,128)}), f32[128,128]{0,1:T(8,128)}) %all-reduce.9.cloned.1.call-update) | async-done | bytes 65552 | tf_op jit(solution)/shard_map/psum | solution.py:12
  134.2 0.9 copy.33
  135.1 0.9 fusion.48
  135.9 11.7 cholesky.44
  147.7 0.6 compare_reduce_fusion.1
  148.3 0.7 select_bitcast_fusion.1
  149.0 9.8 custom-call.6
  158.8 0.3 fusion.37
  159.2 1.2 fusion.1
  160.6 0.7 fusion.2
  161.3 309.4 %all-reduce.11.cloned.1.call-done = f32[6,128,128]{1,2,0:T(8,128)} async-done(((f32[6,128,128]{1,2,0:T(8,128)}), f32[6,128,128]{1,2,0:T(8,128)}) %all-reduce.11.cloned.1.call-update) | async-done | bytes 393232 | tf_op jit(solution)/shard_map/psum | solution.py:12
  470.7 1.6 gather_fusion
  472.2 0.8 select_select_fusion.1
  473.1 0.7 broadcast_and_fusion.1
  473.8 118.5 %all-reduce.13.cloned.1.call-done = f32[3,128,128]{1,2,0:T(8,128)} async-done(((f32[3,128,128]{1,2,0:T(8,128)}), f32[3,128,128]{1,2,0:T(8,128)}) %all-reduce.13.cloned.1.call-update) | async-done | bytes 196624 | tf_op jit(solution)/shard_map/psum | solution.py:12
  592.2 2.3 convolution_subtract_fusion.1
  594.6 0.6 fusion.41
  595.2 0.2 all-reduce.17.cloned.1.call-start
  595.5 1.7 convolution_reduce_fusion.1
  597.2 115.8 %all-reduce.15.cloned.1.call-done = f32[128,128]{0,1:T(8,128)} async-done(((f32[128,128]{0,1:T(8,128)}), f32[128,128]{0,1:T(8,128)}) %all-reduce.15.cloned.1.call-update) | async-done | bytes 65552 | tf_op jit(solution)/shard_map/psum | solution.py:12
  712.9 0.9 copy.42
  713.9 0.9 fusion.45
  714.7 11.7 cholesky.55
  726.5 0.6 compare_reduce_fusion
  727.1 0.7 select_bitcast_fusion
  727.8 9.8 custom-call.7
  737.6 0.3 fusion.35
  738.0 1.2 fusion
  739.4 0.8 fusion.7
  740.2 309.2 %all-reduce.17.cloned.1.call-done = f32[6,128,128]{1,2,0:T(8,128)} async-done(((f32[6,128,128]{1,2,0:T(8,128)}), f32[6,128,128]{1,2,0:T(8,128)}) %all-reduce.17.cloned.1.call-update) | async-done | bytes 393232 | tf_op jit(solution)/shard_map/psum | solution.py:12
  1049.4 1.7 gather_fusion.1
  1051.2 0.8 select_select_fusion
  1052.0 119.1 %all-reduce.19.cloned.1.call-done = f32[3,128,128]{1,2,0:T(8,128)} async-done(((f32[3,128,128]{1,2,0:T(8,128)}), f32[3,128,128]{1,2,0:T(8,128)}) %all-reduce.19.cloned.1.call-update) | async-done | bytes 196624 | tf_op jit(solution)/shard_map/psum | solution.py:12
  1171.1 2.2 convolution_subtract_fusion
  1173.4 0.6 copy-done.15
  1174.1 0.1 fusion.93
  1174.3 0.5 copy-done.14
  1174.8 1.1 convolution_reduce_fusion
  1176.0 30.0 %all-reduce.1 = (f32[3,128]{1,0:T(4,128)S(1)}, f32[3,128]{1,0:T(4,128)S(1)}) all-reduce(f32[3,128]{1,0:T(4,128)S(1)} %bitcast.205, f32[3,128]{1,0:T(4,128)S(1)} %bitcast.206), channel_id=1, replica_groups=mesh['prow'=16,'pcol'=32] {'prow'}, use_global_device_ids=true, to_apply=%region_8.12 | all-reduce | flops 768 | bytes 6144 | tf_op jit(solution)/shard_map/psum | solution.py:44
  1206.0 0.2 fusion.5
  1206.2 83.8 %psum.105 = f32[128]{0:T(128)S(1)} all-reduce(f32[128]{0:T(128)S(1)} %fusion.5), channel_id=1, replica_groups=mesh['prow'=16,'pcol'=32] {'pcol'}, use_global_device_ids=true, to_apply=%region_9.13 | all-reduce | flops 128 | bytes 1024 | tf_op jit(solution)/shard_map/psum | solution.py:12
  1290.0 0.2 fusion.71
  1290.3 0.2 fusion.4
  1290.5 0.8 fusion.56
  1291.3 2.6 copy.50
  1294.0 0.3 fusion.6
  1294.2 78.9 %all-reduce = (f32[128]{0:T(128)S(1)}, f32[6,128]{1,0:T(8,128)S(1)}, f32[128]{0:T(128)S(1)}, f32[128]{0:T(128)S(1)}, f32[6,128]{1,0:T(8,128)S(1)}) all-reduce(f32[128]{0:T(128)S(1)} %fusion.4, f32[6,128]{1,0:T(8,128)S(1)} %bitcast.203, f32[128]{0:T(128)S(1)} %fusion.6, ...), channel_id=1, replica_groups=mesh['prow'=16,'pcol'=32] {'pcol'}, use_global_device_ids=true, to_apply=%region_10.14 | all-reduce | flops 1920 | bytes 15360 | tf_op jit(solution)/shard_map/psum | solution.py:12
  1373.2 0.2 fusion.68
  1373.5 0.6 reshape.358
  1374.1 0.6 abs_reduce_fusion.1
  1374.7 0.3 fusion.66
  1375.0 0.3 fusion.64
  1375.3 0.7 abs_reduce_fusion
  1376.0 0.6 reshape.359
  (95 shorter events, 1.4 us)
Async XLA Ops:
  7.2 127.0 %all-reduce.9.cloned.1.call-start = ((), (), s32[]{:S(2)}) async-start(), calls=%async_computation | async-start | bytes 131072 | tf_op jit(solution)/shard_map/psum | solution.py:12
  9.6 1.7 copy-start.7
  12.1 3.1 copy-start.12
  14.5 456.2 %all-reduce.11.cloned.1.call-start = ((), (), s32[]{:S(2)}) async-start(), calls=%async_computation.1 | async-start | bytes 786432 | tf_op jit(solution)/shard_map/psum | solution.py:12
  14.6 1.3 copy-start.20
  14.6 458.5 %copy-start.18 = (pred[3]{0:T(512)(128)(4,1)}, pred[3]{0:T(512)(128)(4,1)S(1)}, u32[]{:S(2)}) copy-start(pred[3]{0:T(512)(128)(4,1)S(1)} %broadcast_compare_fusion.3) | copy-start | bytes 13
  14.6 146.6 %copy-start.29 = (pred[6]{0:T(512)(128)(4,1)}, pred[6]{0:T(512)(128)(4,1)S(1)}, u32[]{:S(2)}) copy-start(pred[6]{0:T(512)(128)(4,1)S(1)} %get-tuple-element.81) | copy-start | bytes 22
  15.2 457.9 %copy-start.27 = (pred[6]{0:T(512)(128)(4,1)}, pred[6]{0:T(512)(128)(4,1)S(1)}, u32[]{:S(2)}) copy-start(pred[6]{0:T(512)(128)(4,1)S(1)} %get-tuple-element.84) | copy-start | bytes 22
  15.9 456.4 %copy-start.24 = (pred[3]{0:T(512)(128)(4,1)}, pred[3]{0:T(512)(128)(4,1)S(1)}, u32[]{:S(2)}) copy-start(pred[3]{0:T(512)(128)(4,1)S(1)} %compare_and_fusion) | copy-start | bytes 13
  159.1 2.2 copy-start.8
  160.5 431.8 %all-reduce.13.cloned.1.call-start = ((), (), s32[]{:S(2)}) async-start(), calls=%async_computation.2 | async-start | bytes 393216 | tf_op jit(solution)/shard_map/psum | solution.py:12
  160.6 313.2 %copy-start.17 = (s32[1024]{0:T(1024)}, s32[1024]{0:T(1024)S(1)}, u32[]{:S(2)}) copy-start(s32[1024]{0:T(1024)S(1)} %pad_clamp_fusion) | copy-start | bytes 12292
  473.0 239.9 %all-reduce.15.cloned.1.call-start = ((), (), s32[]{:S(2)}) async-start(), calls=%async_computation.3 | async-start | bytes 131072 | tf_op jit(solution)/shard_map/psum | solution.py:12
  473.8 121.7 %copy-start.13 = (s32[6,1,128]{2,1,0:T(1,128)S(1)}, s32[6,1,128]{2,1,0:T(1,128)}, u32[]{:S(2)}) copy-start(s32[6,1,128]{2,1,0:T(1,128)} %param.20) | copy-start | bytes 9220
  594.6 143.4 %copy-start.23 = (pred[6]{0:T(512)(128)(4,1)S(1)}, pred[6]{0:T(512)(128)(4,1)}, u32[]{:S(2)}) copy-start(pred[6]{0:T(512)(128)(4,1)} %get-tuple-element.83) | copy-start | bytes 22
  594.6 143.4 %copy-start.28 = (pred[6]{0:T(512)(128)(4,1)S(1)}, pred[6]{0:T(512)(128)(4,1)}, u32[]{:S(2)}) copy-start(pred[6]{0:T(512)(128)(4,1)} %copy-done.27) | copy-start | bytes 22
  595.2 454.2 %all-reduce.17.cloned.1.call-start = ((), (), s32[]{:S(2)}) async-start(), calls=%async_computation.4 | async-start | bytes 786432 | tf_op jit(solution)/shard_map/psum | solution.py:12
  597.2 142.2 %copy-start.5 = (f32[3,128,128]{1,2,0:T(8,128)S(1)}, f32[3,128,128]{1,2,0:T(8,128)}, u32[]{:S(2)}) copy-start(f32[3,128,128]{1,2,0:T(8,128)} %all-reduce.13.cloned.1.call-done) | copy-start | bytes 589828
  737.9 1.4 copy-start.10
  738.0 313.2 %copy-start.25 = (pred[3]{0:T(512)(128)(4,1)S(1)}, pred[3]{0:T(512)(128)(4,1)}, u32[]{:S(2)}) copy-start(pred[3]{0:T(512)(128)(4,1)} %copy-done.24) | copy-start | bytes 13
  739.3 312.7 %copy-start.2 = (f32[6,128,128]{1,2,0:T(8,128)S(1)}, f32[6,128,128]{1,2,0:T(8,128)}, u32[]{:S(2)}) copy-start(f32[6,128,128]{1,2,0:T(8,128)} %all-reduce.11.cloned.1.call-done) | copy-start | bytes 1179652
  739.3 431.8 %all-reduce.19.cloned.1.call-start = ((), (), s32[]{:S(2)}) async-start(), calls=%async_computation.5 | async-start | bytes 393216 | tf_op jit(solution)/shard_map/psum | solution.py:12
  740.2 430.9 %copy-start.19 = (pred[3]{0:T(512)(128)(4,1)S(1)}, pred[3]{0:T(512)(128)(4,1)}, u32[]{:S(2)}) copy-start(pred[3]{0:T(512)(128)(4,1)} %copy-done.18) | copy-start | bytes 13
  740.2 430.9 %copy-start.22 = (pred[6,3]{1,0:T(8,128)(4,1)S(1)}, pred[6,3]{1,0:T(8,128)(4,1)}, u32[]{:S(2)}) copy-start(pred[6,3]{1,0:T(8,128)(4,1)} %broadcast_and_fusion) | copy-start | bytes 58
  1049.4 121.7 %copy-start = (f32[6,128,128]{1,2,0:T(8,128)S(1)}, f32[6,128,128]{1,2,0:T(8,128)}, u32[]{:S(2)}) copy-start(f32[6,128,128]{1,2,0:T(8,128)} %all-reduce.17.cloned.1.call-done) | copy-start | bytes 1179652
  1173.3 0.7 copy-start.15
  1174.1 0.7 copy-start.14
  1174.3 1.6 copy-start.16
  1174.3 31.7 %copy-start.9 = (f32[128,128]{1,0:T(8,128)S(1)}, f32[128,128]{1,0:T(8,128)}, u32[]{:S(2)}) copy-start(f32[128,128]{1,0:T(8,128)} %copy-done.8) | copy-start | bytes 196612
  1174.3 115.7 %copy-start.6 = (f32[3,128,128]{1,2,0:T(8,128)S(1)}, f32[3,128,128]{1,2,0:T(8,128)}, u32[]{:S(2)}) copy-start(f32[3,128,128]{1,2,0:T(8,128)} %all-reduce.13.cloned.1.call-done) | copy-start | bytes 589828
  1174.3 115.9 %copy-start.21 = (pred[3]{0:T(512)(128)(4,1)S(1)}, pred[3]{0:T(512)(128)(4,1)}, u32[]{:S(2)}) copy-start(pred[3]{0:T(512)(128)(4,1)} %copy-done.20) | copy-start | bytes 13
  1174.3 116.0 %copy-start.11 = (f32[128,128]{1,0:T(8,128)S(1)}, f32[128,128]{1,0:T(8,128)}, u32[]{:S(2)}) copy-start(f32[128,128]{1,0:T(8,128)} %copy-done.10) | copy-start | bytes 196612
  1291.2 2.7 copy-start.4
  1291.2 3.0 copy-start.26
  1291.3 83.5 %copy-start.3 = (f32[6,128,128]{1,2,0:T(8,128)S(1)}, f32[6,128,128]{1,2,0:T(8,128)}, u32[]{:S(2)}) copy-start(f32[6,128,128]{1,2,0:T(8,128)} %all-reduce.11.cloned.1.call-done) | copy-start | bytes 1179652
  1291.3 83.8 %copy-start.1 = (f32[6,128,128]{1,2,0:T(8,128)S(1)}, f32[6,128,128]{1,2,0:T(8,128)}, u32[]{:S(2)}) copy-start(f32[6,128,128]{1,2,0:T(8,128)} %all-reduce.17.cloned.1.call-done) | copy-start | bytes 1179652
Sparse Core Ops, SparseCore 0:
  14.6 119.4 all-reduce.8
  160.6 310.0 all-reduce.10
  474.2 118.0 all-reduce.12
  595.8 117.0 all-reduce.14
  739.4 309.9 all-reduce.16
  1053.0 118.0 all-reduce.18
where the time goes:
time: 1380 us
  waiting for transfers between devices  1090 us (79%)
  blocking collectives  193 us (14%)
  other arithmetic  57.3 us (4%)
  matrix products  15.1 us (1%)
  between operations  14.7 us (1%)
    psum x6, waiting for transfers between devices, broadcast(): return lax.psum(block, axis)  1090 us
    psum x2, blocking collectives, broadcast(): return lax.psum(block, axis)  163 us
    psum x1, blocking collectives, local(): lax.psum(jnp.einsum('ia,iajc->jc', row_weights, blocks, precision=precise...  30 us
  transfers between devices with their start and end apart: 6, of which 6 were waited for; matrix products, arithmetic and copies ran while one was open for 0% of the time, Pallas kernels for 0%

commit v1 on v0

--- a/solution.py
+++ b/solution.py
@@ -7,9 +7,14 @@
 precise = lax.Precision.HIGHEST
 
 
+def _wait_forms(mine_x, mesh_dim):
+    kept_arr = jnp.sum(lax.all_gather(mine_x, mesh_dim), axis=0)
+    return kept_arr
+
+
 def broadcast(block, axis, holder):
     block = jnp.where(lax.axis_index(axis) == holder, block, jnp.zeros_like(block))
-    return lax.psum(block, axis)
+    return _wait_forms(block, axis)
 
 
 def factor_diagonal(diagonal):

time: 1380 us -> 884 us (0.64)
  waiting for transfers between devices: 1090 us -> 507 us
  blocking collectives: 193 us -> 268 us
  other arithmetic: 57.3 us -> 72.1 us
    psum x6 -> x0, waiting for transfers between devices: 1090 us -> none  [broadcast(): return lax.psum(block, axis)]
    all_gather x0 -> x6, waiting for transfers between devices: none -> 507 us  [_wait_forms(): kept_arr = jnp.sum(lax.all_gather(mine_x, mesh_dim), axis=0)]
    all_gather x0 -> x2, blocking collectives: none -> 156 us  [_wait_forms(): kept_arr = jnp.sum(lax.all_gather(mine_x, mesh_dim), axis=0)]
    psum x2 -> x1, blocking collectives: 163 us -> 81.7 us  [local(): lax.psum(jnp.einsum('iajc,jc->ia', blocks, col_weights, precision=precise...]
    reduce_sum x0 -> x8, other arithmetic: none -> 17.3 us  [_wait_forms(): kept_arr = jnp.sum(lax.all_gather(mine_x, mesh_dim), axis=0)]
  transfers between devices with their start and end apart: 6 -> 6, of which waited for: 6 -> 6; matrix products, arithmetic and copies ran while one was open for 0% -> 1% of each run, Pallas kernels for 0% -> 0%
where the time goes in v1:
time: 884 us
  waiting for transfers between devices  507 us (57%)
  blocking collectives  268 us (30%)
  other arithmetic  72.1 us (8%)
  between operations  14.7 us (2%)
  matrix products  14.6 us (2%)
    all_gather x6, waiting for transfers between devices, _wait_forms(): kept_arr = jnp.sum(lax.all_gather(mine_x, mesh_dim), axis=0)  507 us
    all_gather x2, blocking collectives, _wait_forms(): kept_arr = jnp.sum(lax.all_gather(mine_x, mesh_dim), axis=0)  156 us
    psum x1, blocking collectives, local(): lax.psum(jnp.einsum('iajc,jc->ia', blocks, col_weights, precision=precise...  81.7 us
    psum x1, blocking collectives, local(): lax.psum(jnp.einsum('ia,iajc->jc', row_weights, blocks, precision=precise...  29.6 us
    another operation x6, other arithmetic, factor_diagonal(): factor = jnp.linalg.cholesky(diagonal)  24.8 us
    another operation x4, other arithmetic, factor_diagonal(): inverse = jax.scipy.linalg.solve_triangular(factor, identity, lower=True)  20.9 us
  transfers between devices with their start and end apart: 6, of which 6 were waited for; matrix products, arithmetic and copies ran while one was open for 1% of the time, Pallas kernels for 0%

profile of v1, /device:TPU:64, one launch (start us, length us, event | category | flops | bytes accessed | tf_op | source)
XLA Modules:
  0.0 883.7 jit_solution(9732632453904174821)
XLA Ops:
  7.4 0.7 multiply_exponential_fusion
  8.0 0.8 add_bitcast_fusion.2
  8.8 0.7 fusion.30
  9.6 0.2 reshape.373
  9.7 1.4 copy.30
  11.2 1.4 bitcast_add_fusion
  12.6 0.7 fusion.57
  13.5 41.4 %all-gather.17.cloned.1.call-done = f32[16,128,1,128]{3,1,2,0:T(8,128)} async-done(((f32[1,128,1,128]{3,1,2,0:T(8,128)}), f32[16,128,1,128]{3,1,2,0:T(8,128)}) %all-gather.17.cloned.1.call-update) | async-done | bytes 1048592 | tf_op jit(solution)/shard_map/all_gather | solution.py:11
  54.9 1.3 bitcast_reduce_fusion.1
  56.3 11.7 %cholesky.44 = f32[128,128]{1,0:T(8,128)S(1)} custom-call(f32[128,128]{1,0:T(8,128)S(1)} %fusion.63), custom_call_target="Cholesky" | custom-call | tf_op jit(solution)/shard_map/jit(cholesky)/cholesky | solution.py:21
  68.0 0.6 compare_reduce_fusion.1
  68.7 0.7 select_bitcast_fusion.2
  69.3 9.8 %custom-call.6 = f32[1,128,128]{1,2,0:T(8,128)S(1)} custom-call(f32[1,128,128]{2,1,0:T(8,128)S(1)} %get-tuple-element.81), custom_call_target="InvertDiagBlocksLowerTriangular" | custom-call | tf_op jit(solution)/shard_map/jit(_solve_triangular)/triangular_solve | solution.py:23
  79.1 0.3 fusion.52
  79.4 1.3 fusion.1
  80.8 179.4 %all-gather.19.cloned.1.call-done = f32[192,128,128]{2,1,0:T(8,128)} async-done(((f32[6,128,128]{2,1,0:T(8,128)}), f32[192,128,128]{2,1,0:T(8,128)}) %all-gather.19.cloned.1.call-update) | async-done | bytes 12582928 | tf_op jit(solution)/shard_map/all_gather | solution.py:11
  260.3 5.3 reduce_sum.81
  265.5 0.6 gather_fusion
  266.1 0.8 select_select_fusion.1
  267.0 36.6 %all-gather.21.cloned.1.call-done = f32[48,128,128]{2,1,0:T(8,128)} async-done(((f32[3,128,128]{2,1,0:T(8,128)}), f32[48,128,128]{2,1,0:T(8,128)}) %all-gather.21.cloned.1.call-update) | async-done | bytes 3145744 | tf_op jit(solution)/shard_map/all_gather | solution.py:11
  303.6 2.1 reduce_sum.82
  305.6 2.4 convolution_subtract_fusion.1
  308.1 0.6 fusion.56
  308.7 0.2 all-gather.25.cloned.1.call-start
  309.0 37.7 %all-gather.23.cloned.1.call-done = f32[16,128,1,128]{3,1,2,0:T(8,128)} async-done(((f32[1,128,1,128]{3,1,2,0:T(8,128)}), f32[16,128,1,128]{3,1,2,0:T(8,128)}) %all-gather.23.cloned.1.call-update) | async-done | bytes 1048592 | tf_op jit(solution)/shard_map/all_gather | solution.py:11
  346.7 1.3 bitcast_reduce_fusion
  348.1 11.7 %cholesky.55 = f32[128,128]{1,0:T(8,128)S(1)} custom-call(f32[128,128]{1,0:T(8,128)S(1)} %fusion.60), custom_call_target="Cholesky" | custom-call | tf_op jit(solution)/shard_map/jit(cholesky)/cholesky | solution.py:21
  359.9 0.6 compare_reduce_fusion
  360.5 0.7 select_bitcast_fusion.1
  361.2 9.8 %custom-call.7 = f32[1,128,128]{1,2,0:T(8,128)S(1)} custom-call(f32[1,128,128]{2,1,0:T(8,128)S(1)} %get-tuple-element.79), custom_call_target="InvertDiagBlocksLowerTriangular" | custom-call | tf_op jit(solution)/shard_map/jit(_solve_triangular)/triangular_solve | solution.py:23
  371.0 0.3 fusion.50
  371.3 1.2 fusion
  372.6 179.5 %all-gather.25.cloned.1.call-done = f32[192,128,128]{2,1,0:T(8,128)} async-done(((f32[6,128,128]{2,1,0:T(8,128)}), f32[192,128,128]{2,1,0:T(8,128)}) %all-gather.25.cloned.1.call-update) | async-done | bytes 12582928 | tf_op jit(solution)/shard_map/all_gather | solution.py:11
  552.1 5.3 reduce_sum.85
  557.4 0.6 gather_fusion.1
  557.9 0.8 select_select_fusion
  558.8 0.7 fusion.5
  559.4 0.6 copy.82
  560.0 1.0 fusion.2
  561.2 0.6 broadcast_and_fusion
  561.8 0.7 broadcast_and_fusion.1
  562.4 0.8 fusion.13
  563.3 32.1 %all-gather.27.cloned.1.call-done = f32[48,128,128]{2,1,0:T(8,128)} async-done(((f32[3,128,128]{2,1,0:T(8,128)}), f32[48,128,128]{2,1,0:T(8,128)}) %all-gather.27.cloned.1.call-update) | async-done | bytes 3145744 | tf_op jit(solution)/shard_map/all_gather | solution.py:11
  595.4 2.1 reduce_sum.86
  597.4 1.9 convolution_subtract_fusion
  599.5 0.5 copy-done.9
  600.0 0.7 fusion.16
  600.8 29.6 %all-reduce.1 = (f32[3,128]{1,0:T(4,128)S(1)}, f32[3,128]{1,0:T(4,128)}) all-reduce(f32[3,128]{1,0:T(4,128)S(1)} %bitcast.207, f32[3,128]{1,0:T(4,128)S(1)} %bitcast.208), channel_id=1, replica_groups=mesh['prow'=16,'pcol'=32] {'prow'}, use_global_device_ids=true, to_apply=%region_8.12 | all-reduce | flops 768 | bytes 6144 | tf_op jit(solution)/shard_map/psum | solution.py:49
  630.4 0.2 fusion.10
  630.6 81.4 %all-gather.8 = f32[32,1,128]{2,1,0:T(1,128)S(1)} all-gather(f32[1,1,128]{2,1,0:T(1,128)S(1)} %fusion.10), channel_id=8, replica_groups=mesh['prow'=16,'pcol'=32] {'pcol'}, dimensions={0}, use_global_device_ids=true | all-gather | bytes 16896 | tf_op jit(solution)/shard_map/all_gather | solution.py:11
  712.0 0.3 fusion.86
  712.4 0.2 fusion.11
  712.6 1.2 fusion.14
  713.8 0.2 fusion.12
  714.2 74.9 %all-gather.9 = f32[32,1,128]{2,1,0:T(1,128)S(1)} all-gather(f32[1,1,128]{2,1,0:T(1,128)S(1)} %fusion.11), channel_id=9, replica_groups=mesh['prow'=16,'pcol'=32] {'pcol'}, dimensions={0}, use_global_device_ids=true | all-gather | bytes 16896 | tf_op jit(solution)/shard_map/all_gather | solution.py:11
  789.1 0.3 fusion.83
  789.6 81.7 %all-reduce = (f32[6,128]{1,0:T(8,128)S(1)}, f32[128]{0:T(128)S(1)}, f32[128]{0:T(128)S(1)}, f32[6,128]{1,0:T(8,128)S(1)}) all-reduce(f32[6,128]{1,0:T(8,128)S(1)} %bitcast.205, f32[128]{0:T(128)S(1)} %fusion.12, f32[128]{0:T(128)S(1)} %copy-done.12, f32[6,128]{1,0:T(8,128)S(1)} %bitcast.206), channel_id=1, replica_groups=mesh['prow'=16,'pcol'=32] {'pcol'}, use_global_device_ids=true, to_apply=%region_11.15 | all-reduce | flops 1792 | bytes 14336 | tf_op jit(solution)/shard_map/psum | solution.py:50
  871.3 0.4 fusion.81
  871.8 0.4 fusion.79
  872.2 0.7 abs_reduce_fusion
  872.9 0.6 reshape.376
  873.5 0.6 abs_reduce_fusion.1
  874.1 0.6 copy.40
  874.6 2.2 copy.39
  (88 shorter events, 1.6 us)
Async XLA Ops:
  7.2 47.7 %all-gather.17.cloned.1.call-start = ((), (), s32[]{:S(2)}) async-start(), calls=%async_computation | async-start | bytes 1114112 | tf_op jit(solution)/shard_map/all_gather | solution.py:11
  9.7 1.4 copy-start
  12.6 68.1 %copy-start.1 = (f32[6,128,3,128]{3,1,0,2:T(8,128)}, f32[6,128,3,128]{3,1,0,2:T(8,128)S(1)}, u32[]{:S(2)}) copy-start(f32[6,128,3,128]{3,1,0,2:T(8,128)S(1)} %bitcast_add_fusion) | copy-start | bytes 3538948
  13.4 246.9 %all-gather.19.cloned.1.call-start = ((), (), s32[]{:S(2)}) async-start(), calls=%async_computation.1 | async-start | bytes 12976128 | tf_op jit(solution)/shard_map/all_gather | solution.py:11
  13.4 67.3 %copy-start.19 = (pred[6]{0:T(512)(128)(4,1)}, pred[6]{0:T(512)(128)(4,1)S(1)}, u32[]{:S(2)}) copy-start(pred[6]{0:T(512)(128)(4,1)S(1)} %get-tuple-element.86) | copy-start | bytes 22
  79.4 186.1 %copy-start.2 = (f32[128,128]{1,0:T(8,128)}, f32[128,128]{1,0:T(8,128)S(1)}, u32[]{:S(2)}) copy-start(f32[128,128]{1,0:T(8,128)S(1)} %fusion.52) | copy-start | bytes 196612
  80.7 222.8 %all-gather.21.cloned.1.call-start = ((), (), s32[]{:S(2)}) async-start(), calls=%async_computation.2 | async-start | bytes 3342336 | tf_op jit(solution)/shard_map/all_gather | solution.py:11
  266.9 79.8 %all-gather.23.cloned.1.call-start = ((), (), s32[]{:S(2)}) async-start(), calls=%async_computation.3 | async-start | bytes 1114112 | tf_op jit(solution)/shard_map/all_gather | solution.py:11
  267.0 38.7 %copy-start.16 = (pred[3]{0:T(512)(128)(4,1)}, pred[3]{0:T(512)(128)(4,1)S(1)}, u32[]{:S(2)}) copy-start(pred[3]{0:T(512)(128)(4,1)S(1)} %broadcast_compare_fusion) | copy-start | bytes 13
  308.7 243.3 %all-gather.25.cloned.1.call-start = ((), (), s32[]{:S(2)}) async-start(), calls=%async_computation.4 | async-start | bytes 12976128 | tf_op jit(solution)/shard_map/all_gather | solution.py:11
  309.0 63.5 %copy-start.11 = (pred[6]{0:T(512)(128)(4,1)}, pred[6]{0:T(512)(128)(4,1)S(1)}, u32[]{:S(2)}) copy-start(pred[6]{0:T(512)(128)(4,1)S(1)} %get-tuple-element.87) | copy-start | bytes 22
  309.0 63.5 %copy-start.21 = (pred[6]{0:T(512)(128)(4,1)}, pred[6]{0:T(512)(128)(4,1)S(1)}, u32[]{:S(2)}) copy-start(pred[6]{0:T(512)(128)(4,1)S(1)} %get-tuple-element.88) | copy-start | bytes 22
  371.3 180.8 %copy-start.4 = (f32[128,128]{1,0:T(8,128)}, f32[128,128]{1,0:T(8,128)S(1)}, u32[]{:S(2)}) copy-start(f32[128,128]{1,0:T(8,128)S(1)} %fusion.50) | copy-start | bytes 196612
  372.5 222.8 %all-gather.27.cloned.1.call-start = ((), (), s32[]{:S(2)}) async-start(), calls=%async_computation.5 | async-start | bytes 3342336 | tf_op jit(solution)/shard_map/all_gather | solution.py:11
  552.1 6.7 copy-start.7
  557.4 2.7 copy-start.6
  558.7 2.4 copy-start.17
  558.7 2.4 copy-start.20
  558.8 3.0 copy-start.22
  561.1 0.6 copy-start.13
  599.3 0.7 copy-start.9
  599.3 1.4 copy-start.8
  599.3 31.1 %copy-start.3 = (f32[128,128]{1,0:T(8,128)S(1)}, f32[128,128]{1,0:T(8,128)}, u32[]{:S(2)}) copy-start(f32[128,128]{1,0:T(8,128)} %copy-done.2) | copy-start | bytes 196612
  599.3 113.0 %copy-start.18 = (pred[3]{0:T(512)(128)(4,1)S(1)}, pred[3]{0:T(512)(128)(4,1)}, u32[]{:S(2)}) copy-start(pred[3]{0:T(512)(128)(4,1)} %copy-done.16) | copy-start | bytes 13
  599.4 113.0 %copy-start.5 = (f32[128,128]{1,0:T(8,128)S(1)}, f32[128,128]{1,0:T(8,128)}, u32[]{:S(2)}) copy-start(f32[128,128]{1,0:T(8,128)} %copy-done.4) | copy-start | bytes 196612
  600.7 113.3 %copy-start.10 = (pred[6,3]{0,1:T(4,128)(4,1)S(1)}, pred[6,3]{0,1:T(4,128)(4,1)}, u32[]{:S(2)}) copy-start(pred[6,3]{0,1:T(4,128)(4,1)} %broadcast_and_fusion.1) | copy-start | bytes 58
  714.1 75.4 %copy-start.14 = (pred[3]{0:T(512)(128)(4,1)S(1)}, pred[3]{0:T(512)(128)(4,1)}, u32[]{:S(2)}) copy-start(pred[3]{0:T(512)(128)(4,1)} %copy-done.13) | copy-start | bytes 13
  714.1 75.6 %copy-start.12 = (f32[128]{0:T(128)S(1)}, f32[128]{0:T(128)}, u32[]{:S(2)}) copy-start(f32[128]{0:T(128)} %fusion.13) | copy-start | bytes 1540
  714.1 159.4 %copy-start.15 = (f32[3,128]{1,0:T(4,128)S(1)}, f32[3,128]{1,0:T(4,128)}, u32[]{:S(2)}) copy-start(f32[3,128]{1,0:T(4,128)} %get-tuple-element.76) | copy-start | bytes 4612
Sparse Core Ops, SparseCore 0:
  13.5 41.3 all-gather.16
  80.8 179.3 all-gather.18
  267.0 36.4 all-gather.20
  308.9 37.8 all-gather.22
  372.7 179.3 all-gather.24
  558.8 36.4 all-gather.26
